TPU v7x, 32 devices: a whole 2x2x4 slice. The times are simulated.
32 devices in a mesh: ctx: 8 (over z, y), head: 4 (over x, core).
Axes of the slice: x: 2, y: 2, z: 4, core: 2. Of those that a mesh axis runs over, the one named last changes fastest.
Arguments:
- tokens: bfloat16 [4096, 1024], P('ctx'), may hold values from -24 to 24
- w_query: bfloat16 [1024, 1024], P(None, 'head'), may hold values from -0.1875 to 0.1875
- w_key: bfloat16 [1024, 1024], P(None, 'head'), may hold values from -0.1875 to 0.1875
- w_value: bfloat16 [1024, 1024], P(None, 'head'), may hold values from -0.1875 to 0.1875
- w_out: bfloat16 [1024, 1024], P('head'), may hold values from -0.1875 to 0.1875
- block_mask: int32 [32, 32], replicated, may hold values from 0 to 1, as said below
- block_order: int32 [32], replicated, may hold values from 0 to 31, each once
Outputs:
- mixed: bfloat16 [4096, 1024], P('ctx', 'head')
Inputs may be any that keep to these rules, and one draw needn't show every extreme that they name: `block_mask`: entries are 0 or 1 and every diagonal entry is 1. `block_order`: each initial block index appears once.
All inputs are finite; a program needn't handle non-finite values.
Results may differ from a plain program's by a relative error of at most 0.013.
Values may be sent and summed in bfloat16 or wider, within the bound.
No kernel may reach another device: no remote copies, remote signals or barrier semaphores. Data moves between devices by JAX's collectives and lax.ppermute only.
A program may use at most 256 MiB of HBM per device.

v0:
```python
import functools

import jax
import jax.numpy as jnp
from jax import lax
from jax.experimental import pallas as pl
from jax.experimental.pallas import tpu as pltpu
from jax.sharding import PartitionSpec as P


HEAD_DIM = 64
BLOCK = 128
LANES = 128
SLOTS = 4
STREAMS = 4
TALL = HEAD_DIM + 16
NEG = -1e30


HBM = pl.BlockSpec(memory_space=pltpu.HBM)
VMEM = pl.BlockSpec(memory_space=pltpu.VMEM)
SMEM = pl.BlockSpec(memory_space=pltpu.SMEM)
GRANT = 16 * 1024 * 1024
WHOLE = 60 * 1024 * 1024


def low_half(shape):
    return lax.broadcasted_iota(jnp.int32, shape, len(shape) - 1) < HEAD_DIM


def swap_halves(x):
    return pltpu.roll(x, HEAD_DIM, 1)


def proj_kernel(inner, heads, near, tok_in, wk_in, wv_in, wq_in, *rest):
    n_out = 2 * heads - near
    outs, (tok, wk, wv, wq, msg, sems) = rest[:n_out], rest[n_out:]
    loads = [
        pltpu.make_async_copy(src, dst, sems.at[n])
        for n, (src, dst) in enumerate(((tok_in, tok), (wv_in, wv), (wk_in, wk), (wq_in, wq)))
    ]
    for load in loads:
        load.start()
    a = lax.axis_index("ctx") // inner
    rows = tok.shape[0]
    half = rows // 2
    low = low_half((half, LANES))
    loads[0].wait()
    loads[1].wait()
    v = jnp.dot(tok[...], wv[...], preferred_element_type=jnp.float32)
    loads[2].wait()
    loads[3].wait()
    q = jnp.dot(tok[...], wq[...], preferred_element_type=jnp.float32) * HEAD_DIM ** (-0.5)
    k = jnp.dot(tok[...], wk[...], preferred_element_type=jnp.float32)
    for base, x in ((half, v), (rows, q)):
        for g in range(heads // 2):
            for i in range(rows // BLOCK):
                block = x[i * BLOCK : (i + 1) * BLOCK, g * LANES : (g + 1) * LANES]
                turned = jnp.transpose(block).astype(jnp.bfloat16)
                start = base + i * HEAD_DIM
                msg[2 * g, start : start + HEAD_DIM] = turned[:HEAD_DIM]
                msg[2 * g + 1, start : start + HEAD_DIM] = turned[HEAD_DIM:]
    for h in range(heads):
        cols = slice(LANES * (h // 2), LANES * (h // 2) + LANES)
        top, bottom = k[:half, cols], k[half:, cols]
        if h % 2 == 0:
            bottom = swap_halves(bottom)
        else:
            top = swap_halves(top)
        msg[h, :half] = jnp.where(low, top, bottom).astype(jnp.bfloat16)
    for j in range(heads):
        if j < near:
            outs[j][...] = msg[a ^ j]
        else:
            outs[j][...] = msg[a ^ j, :rows]
            outs[heads + j - near][...] = msg[a ^ j, rows:]


def list_kernel(inner, outer, per, cap, parts, mask, order, who, where, which, valid, first, steps, names, ends, load):
    c = lax.axis_index("ctx")
    a = c // inner
    b = (c % inner) // 2 * 2 + lax.axis_index("head") % 2
    blocks = inner * outer * per
    half = per // 2
    size = outer * per // parts
    span = blocks + SLOTS

    def name(dev, _):
        kb = ((lax.div(dev, inner) ^ a) * inner + (lax.rem(dev, inner) ^ b)) * per
        for i in range(per):
            names[dev * per + i] = order[kb + i // 2 + i % 2 * half]
        return 0

    lax.fori_loop(0, inner * outer, name, 0)

    def piece(k, _):
        qb = ((k ^ a) * inner + b) * per
        own = [order[qb + i] for i in range(per)]

        def col(n, to):
            to = list(to)
            for e in range(8):
                slot = n * 8 + e
                key = names[slot]
                for i in range(per):
                    which[to[i]] = slot
                    to[i] = to[i] + mask[own[i], key]
            return tuple(to)

        begin = [(k * per + i) * span for i in range(per)]
        end = lax.fori_loop(0, blocks // 8, col, tuple(begin))
        for i in range(per):
            keep = which[begin[i]]
            for extra in range(SLOTS):
                which[end[i] + extra] = keep
            ends[k * per + i] = end[i]
        return 0

    lax.fori_loop(0, outer, piece, 0)
    for part in range(parts):
        for s in range(STREAMS):
            load[s] = 0

        def row(qi, _):
            s, least = jnp.int32(0), load[0]
            for other in range(1, STREAMS):
                here = load[other]
                s = jnp.where(here < least, other, s)
                least = jnp.minimum(here, least)
            item = (part * STREAMS + s) * cap + least
            start = qi * span
            count = ends[qi] - start
            items = lax.div(count + (SLOTS - 1), SLOTS)

            def mark(t, left):
                who[item + t] = qi - part * size
                where[item + t] = start + t * SLOTS
                valid[item + t] = left
                first[item + t] = 0
                return left - SLOTS

            lax.fori_loop(0, items, mark, count)
            first[item] = 1
            load[s] = least + items
            return 0

        lax.fori_loop(part * size, (part + 1) * size, row, 0)
        most = load[0]
        for s in range(1, STREAMS):
            most = jnp.maximum(most, load[s])
        steps[part] = most
        for s in range(STREAMS):
            start = (part * STREAMS + s) * cap
            last = start + jnp.maximum(load[s] - 1, 0)
            idle = load[s] == 0
            qi = jnp.where(idle, size, who[last])
            key = jnp.where(idle, 0, where[last])

            def fill(t, _):
                who[start + t] = qi
                where[start + t] = key
                valid[start + t] = 0
                first[start + t] = 0
                return 0

            lax.fori_loop(load[s], most + 2, fill, 0)


def attend_kernel(part, per, cap, n_kv, spans, who, where, which, valid, first, steps, *rest):
    ins, rest = rest[:n_kv], rest[n_kv:]
    q_in, rest = rest[: len(spans)], rest[len(spans) :]
    outs, rest = rest[: len(spans)], rest[len(spans) :]
    if part == 0:
        (kq, vt), rest = rest[:2], rest[2:]
    else:
        kq, vt = ins
    qt, sc, m_s, al_s, acc_s, acc_all = rest
    half = per // 2
    nq = len(spans) * per
    zero = jnp.zeros((HEAD_DIM, BLOCK), jnp.bfloat16)
    ones = jnp.ones((TALL - HEAD_DIM, BLOCK), jnp.bfloat16)
    for k, start in enumerate(spans):
        for i in range(per):
            turned = q_in[k][start + i * HEAD_DIM : start + (i + 1) * HEAD_DIM, :]
            qt[0, k * per + i] = jnp.concatenate([turned, zero], axis=0)
            qt[1, k * per + i] = jnp.concatenate([zero, turned], axis=0)
    qt[:, nq] = jnp.zeros((2, LANES, BLOCK), jnp.bfloat16)
    if part == 0:
        for n, msg in enumerate(ins):
            for r in range(half):
                kq[n * half + r] = msg[r * BLOCK : (r + 1) * BLOCK, :]
            for i in range(per):
                start = half * BLOCK + (i // 2 + i % 2 * half) * HEAD_DIM
                vt[n * per + i, :HEAD_DIM] = msg[start : start + HEAD_DIM, :]
                vt[n * per + i, HEAD_DIM:] = ones
    m_s[...] = jnp.full(m_s.shape, NEG, jnp.float32)
    acc_s[...] = jnp.zeros(acc_s.shape, jnp.float32)

    def keys(s, t):
        start = where[(part * STREAMS + s) * cap + t]
        return [which[start + e] for e in range(SLOTS)]

    def score(t, buf, s):
        qi = who[(part * STREAMS + s) * cap + t]
        tiles = []
        for e, slot in enumerate(keys(s, t)):
            tile = jnp.dot(kq[slot >> 1], qt[slot & 1, qi], preferred_element_type=jnp.float32)
            sc[buf, s, e] = tile
            tiles.append(tile.reshape(BLOCK // 8, 8, BLOCK))
        top = jnp.max(functools.reduce(jnp.maximum, tiles), axis=0)
        top = jnp.max(top, axis=0, keepdims=True)
        m_old = jnp.where(first[(part * STREAMS + s) * cap + t] == 1, NEG, m_s[1 - buf, s])
        m_new = jnp.maximum(m_old, top)
        al_s[buf, s] = jnp.exp(m_old - m_new)
        m_s[buf, s] = m_new

    def weigh(t, buf, s):
        qi = who[(part * STREAMS + s) * cap + t]
        n_valid = valid[(part * STREAMS + s) * cap + t]
        m, alpha = m_s[buf, s], al_s[buf, s]
        acc = acc_s[s] * alpha
        ids = keys(s, t)
        for e in range(0, SLOTS, 2):
            probs = []
            for f in (e, e + 1):
                shut = m + jnp.where(f < n_valid, 0.0, -NEG)
                probs.append(jnp.exp(sc[buf, s, f] - shut).astype(jnp.bfloat16))
            acc = acc + jnp.dot(
                jnp.concatenate([vt[ids[e]], vt[ids[e + 1]]], axis=1),
                jnp.concatenate(probs, axis=0),
                preferred_element_type=jnp.float32,
            )
        acc_s[s] = acc
        acc_all[qi] = acc

    for s in range(STREAMS):
        score(0, 0, s)
    count = steps[part]

    def step(u, _):
        for buf in (0, 1):
            for s in range(STREAMS):
                score(2 * u + 1 + buf, 1 - buf, s)
                weigh(2 * u + buf, buf, s)
        return 0

    lax.fori_loop(0, lax.div(count, 2), step, 0)

    @pl.when(lax.rem(count, 2) == 1)
    def _():
        for s in range(STREAMS):
            weigh(count - 1, 0, s)

    for k in range(len(spans)):
        for r in range(half):
            done = []
            for i in (k * per + r, k * per + r + half):
                total = acc_all[i]
                done.append(total[:HEAD_DIM] * (1.0 / total[HEAD_DIM : HEAD_DIM + 1]))
            outs[k][r * BLOCK : (r + 1) * BLOCK, :] = jnp.transpose(
                jnp.concatenate(done, axis=0)
            ).astype(jnp.bfloat16)


def out_kernel(inner, heads, groups, other, *refs):
    pieces = [refs[g * heads : (g + 1) * heads] for g in range(groups)]
    ws = refs[groups * heads : groups * heads + groups]
    out = refs[-1]
    a = lax.axis_index("ctx") // inner
    side = (lax.axis_index("head") % 2) ^ other
    cols = pl.ds(pl.multiple_of(side * out.shape[1], LANES), out.shape[1])
    half = pieces[0][0].shape[0]
    low = low_half((half, LANES))
    tops, bottoms, rows = [], [], []
    for g in range(groups):
        for k in range(0, heads, 2):
            p0 = pieces[g][k][...].astype(jnp.float32)
            p1 = pieces[g][k + 1][...].astype(jnp.float32)
            tops.append(jnp.where(low, p0, swap_halves(p1)).astype(jnp.bfloat16))
            bottoms.append(jnp.where(low, swap_halves(p0), p1).astype(jnp.bfloat16))
            for e in (0, 1):
                start = pl.multiple_of(HEAD_DIM * (a ^ (k + e)), HEAD_DIM)
                rows.append(ws[g][pl.ds(start, HEAD_DIM), cols])
    w = jnp.concatenate(rows, axis=0)
    for n, parts in enumerate((tops, bottoms)):
        x = jnp.concatenate(parts, axis=1)
        total = jnp.dot(x, w, preferred_element_type=jnp.float32)
        if not other:
            total = total + refs[-2][n * half : (n + 1) * half, :].astype(jnp.float32)
        out[n * half : (n + 1) * half, :] = total.astype(out.dtype)


def solution(mesh):
    ctx, groups = mesh.shape["ctx"], mesh.shape["head"]

    def body(tokens, w_query, w_key, w_value, w_out, block_mask, block_order):
        rows = tokens.shape[0]
        heads = w_query.shape[1] // HEAD_DIM
        inner = ctx // heads
        per = rows // BLOCK
        nb = block_mask.shape[0]
        nq = heads * per
        cols = w_out.shape[1] // groups
        bf = jnp.bfloat16
        params = pltpu.CompilerParams(vmem_limit_bytes=GRANT)
        both = ("ctx", "head")
        places = [(c // inner, c % inner, h) for c in range(ctx) for h in range(groups)]

        def index(a, b, h):
            return (a * inner + b) * groups + h

        def turn(x, j):
            pairs = [
                (index(a, b, h), index(a ^ j, (b & ~1) | (h & 1), (h & ~1) | (b & 1)))
                for a, b, h in places
            ]
            return lax.ppermute(x, both, pairs)

        def spread(x, e):
            pairs = [
                (index(a, b, h), index(a, b ^ (e & ~1), h ^ (e & 1))) for a, b, h in places
            ]
            return lax.ppermute(x, both, pairs) if e else x

        def head_swap(x, j):
            return lax.ppermute(x, "head", [(h, h ^ j) for h in range(groups)]) if j else x

        half, size = rows // 2, rows + rows // 2
        near = heads // 2
        sizes = [size] * near + [rows] * (heads - near) + [half] * (heads - near)
        msgs = pl.pallas_call(
            functools.partial(proj_kernel, inner, heads, near),
            out_shape=[jax.ShapeDtypeStruct((n, LANES), bf) for n in sizes],
            in_specs=[HBM] * 4,
            out_specs=[VMEM] * len(sizes),
            scratch_shapes=[pltpu.VMEM(x.shape, bf) for x in (tokens, w_value, w_key, w_query)]
            + [
                pltpu.VMEM((heads, size, LANES), bf),
                pltpu.SemaphoreType.DMA((4,)),
            ],
            compiler_params=pltpu.CompilerParams(vmem_limit_bytes=WHOLE),
            name="proj",
        )(tokens, w_key, w_value, w_query)
        got, late = [None] * heads, [None] * heads
        for j in reversed(range(heads)):
            got[j] = turn(msgs[j], j)
        parts = heads // near
        longest = -(-nb // SLOTS)
        cap = -(-nq // parts * longest // STREAMS) + longest + 3
        tables = pl.pallas_call(
            functools.partial(list_kernel, inner, heads, per, cap, parts),
            out_shape=[
                jax.ShapeDtypeStruct((parts * STREAMS * cap,), jnp.int32),
                jax.ShapeDtypeStruct((parts * STREAMS * cap,), jnp.int32),
                jax.ShapeDtypeStruct((nq * (nb + SLOTS),), jnp.int32),
                jax.ShapeDtypeStruct((parts * STREAMS * cap,), jnp.int32),
                jax.ShapeDtypeStruct((parts * STREAMS * cap,), jnp.int32),
                jax.ShapeDtypeStruct((parts,), jnp.int32),
            ],
            in_specs=[SMEM] * 2,
            out_specs=[SMEM] * 6,
            scratch_shapes=[
                pltpu.SMEM((nb,), jnp.int32),
                pltpu.SMEM((nq,), jnp.int32),
                pltpu.SMEM((STREAMS,), jnp.int32),
            ],
            name="block_lists",
        )(block_mask, block_order)
        queries = msgs[heads:]
        got[0], tables = lax.optimization_barrier((got[0], tables))
        for j in range(near, heads):
            late[j] = turn(queries[j - near], j)
        kv = []
        for j in range(heads):
            for e in range(inner):
                kv.append(spread(got[j], e))
        o = []
        for part in range(parts):
            if part == 0:
                queries, spans = got[:near], (rows,) * near
                extra = [
                    jax.ShapeDtypeStruct((nb // 2, BLOCK, LANES), bf),
                    jax.ShapeDtypeStruct((nb, TALL, BLOCK), bf),
                ]
            else:
                queries, spans, extra = late[part * near : (part + 1) * near], (0,) * near, []
            mini = near * per + 1
            made = pl.pallas_call(
                functools.partial(attend_kernel, part, per, cap, len(kv), spans),
                out_shape=[jax.ShapeDtypeStruct((half, LANES), bf)] * near + extra,
                in_specs=[SMEM] * 6 + [VMEM] * (len(kv) + near),
                out_specs=[VMEM] * (near + len(extra)),
                scratch_shapes=[
                    pltpu.VMEM((2, mini, LANES, BLOCK), bf),
                    pltpu.VMEM((2, STREAMS, SLOTS, BLOCK, BLOCK), jnp.float32),
                    pltpu.VMEM((2, STREAMS, 1, BLOCK), jnp.float32),
                    pltpu.VMEM((2, STREAMS, 1, BLOCK), jnp.float32),
                    pltpu.VMEM((STREAMS, TALL, BLOCK), jnp.float32),
                    pltpu.VMEM((mini, TALL, BLOCK), jnp.float32),
                ],
                compiler_params=params,
            )(*tables, *kv, *queries)
            o += made[:near]
            if part == 0:
                h = lax.axis_index("head")
                w_out, kv = lax.optimization_barrier((w_out, made[near:]))
                w_cols = []
                for g in range(0, groups, 2):
                    start = (h // 2 ^ g // 2) * 2 * cols
                    share = lax.dynamic_slice_in_dim(w_out, start, 2 * cols, axis=1)
                    w_cols.append(head_swap(share, g))
        mine = [None] * heads
        for j in reversed(range(heads)):
            mine[j] = turn(o[j], j)
        pieces = []
        for g in range(0, groups, 2):
            for j in range(heads):
                pieces.append(head_swap(mine[j], g))

        def out(other, *more):
            return pl.pallas_call(
                functools.partial(out_kernel, inner, heads, groups // 2, other),
                out_shape=jax.ShapeDtypeStruct((rows, cols), bf),
                in_specs=[VMEM] * (len(pieces) + len(w_cols) + len(more)),
                out_specs=VMEM,
                compiler_params=params,
            )(*pieces, *w_cols, *more)

        return out(0, head_swap(out(1), 1))

    placed = (
        P("ctx", None),
        P(None, "head"),
        P(None, "head"),
        P(None, "head"),
        P("head", None),
        P(),
        P(),
    )
    return jax.shard_map(
        body, mesh=mesh, in_specs=placed, out_specs=P("ctx", "head"), check_vma=False
    )
```

profile of v0, /device:TPU:0, one launch (start us, length us, event | category | flops | bytes accessed | tf_op | source)
XLA Modules:
  0.0 61.2 jit_solution(16524692694682838621)
XLA Ops:
  0.0 3.6 %proj.1 = (bf16[768,128]{1,0:T(8,128)(2,1)}, bf16[768,128]{1,0:T(8,128)(2,1)}, bf16[512,128]{1,0:T(8,128)(2,1)}, bf16[512,128]{1,0:T(8,128)(2,1)}, bf16[256,128]{1,0:T(8,128)(2,1)}, /*index=5*/bf16[256,128]{1,0:T(8,128)(2,1)}) custom-call(bf16[512,1024]{1,0:T(8,128)(2,1)} %tok_in.1, bf16[1024,256]{1,0:T(8,128)(2,1)} %wk_in.1, bf16[1024,256]{1,0:T(8,128)(2,1)} %wv_in.1, ...), custom_call_target="tpu_custom_call" | custom-call | tf_op jit(solution)/shard_map/proj/pallas_call | solution.py:331
  3.6 1.6 %collective-permute-start = (bf16[768,128]{1,0:T(8,128)(2,1)}, bf16[768,128]{1,0:T(8,128)(2,1)S(1)}, u32[]{:S(2)}, u32[]{:S(2)}) collective-permute-start(bf16[768,128]{1,0:T(8,128)(2,1)} %get-tuple-element.33), channel_id=1, source_target_pairs={{0,0},{1,4},{2,2},{3,6},{4,1},{5,5},{6,3},{7,7},{8,8},{9,12},{10,1... | collective-permute-start | bytes 589832 | tf_op jit(solution)/shard_map/ppermute | solution.py:317
  5.2 3.1 %collective-permute-start.2 = (bf16[768,128]{1,0:T(8,128)(2,1)}, bf16[768,128]{1,0:T(8,128)(2,1)S(1)}, u32[]{:S(2)}, u32[]{:S(2)}) collective-permute-start(bf16[768,128]{1,0:T(8,128)(2,1)} %get-tuple-element.47), channel_id=1, source_target_pairs={{0,8},{1,12},{2,10},{3,14},{4,9},{5,13},{6,11},{7,15},{8,0},{9,4},... | collective-permute-start | bytes 589832 | tf_op jit(solution)/shard_map/ppermute | solution.py:317
  8.2 2.6 %collective-permute-start.4 = (bf16[512,128]{1,0:T(8,128)(2,1)}, bf16[512,128]{1,0:T(8,128)(2,1)S(1)}, u32[]{:S(2)}, u32[]{:S(2)}) collective-permute-start(bf16[512,128]{1,0:T(8,128)(2,1)} %get-tuple-element.48), channel_id=1, source_target_pairs={{0,16},{1,20},{2,18},{3,22},{4,17},{5,21},{6,19},{7,23},{8,24},{9,... | collective-permute-start | bytes 393224 | tf_op jit(solution)/shard_map/ppermute | solution.py:317
  10.8 0.0 collective-permute-start.6
  10.8 3.9 %block_lists.1 = (s32[216]{0:T(256)}, s32[216]{0:T(256)}, s32[576]{0:T(1024)}, s32[216]{0:T(256)}, s32[216]{0:T(256)}, /*index=5*/s32[2]{0:T(128)}) custom-call(s32[32,32]{1,0:T(8,128)} %mask.1, s32[32]{0:T(128)} %order.1), custom_call_target="tpu_custom_call" | custom-call | tf_op jit(solution)/shard_map/block_lists/pallas_call | solution.py:350
  14.7 0.0 collective-permute-done.rest_0_.rest_8_
  14.7 2.6 %collective-permute-start.1 = (bf16[768,128]{1,0:T(8,128)(2,1)S(1)}, bf16[768,128]{1,0:T(8,128)(2,1)S(1)}, u32[]{:S(2)}, u32[]{:S(2)}) collective-permute-start(bf16[768,128]{1,0:T(8,128)(2,1)S(1)} %collective-permute-done.rest_0_.rest_8_), channel_id=1, source_target_pairs={{0,1},{1,0},{2,3},{3,2},{4,5},{5,4},{6,7},{7,6},{8,9},{9,8},{10,11... | collective-permute-start | bytes 589832 | tf_op jit(solution)/shard_map/ppermute | solution.py:323
  17.4 0.0 collective-permute-done.2.rest_2_.rest_9_
  17.4 0.1 collective-permute-start.3
  17.4 0.0 collective-permute-done.4.rest_4_
  17.4 4.7 %collective-permute-start.5 = (bf16[512,128]{1,0:T(8,128)(2,1)S(1)}, bf16[512,128]{1,0:T(8,128)(2,1)S(1)}, u32[]{:S(2)}, u32[]{:S(2)}) collective-permute-start(bf16[512,128]{1,0:T(8,128)(2,1)S(1)} %collective-permute-done.4.rest_4_), channel_id=1, source_target_pairs={{0,1},{1,0},{2,3},{3,2},{4,5},{5,4},{6,7},{7,6},{8,9},{9,8},{10,11... | collective-permute-start | bytes 393224 | tf_op jit(solution)/shard_map/ppermute | solution.py:323
  22.1 0.0 collective-permute-done.6.rest_6_
  22.1 0.0 collective-permute-start.7
  22.1 0.0 copy-start.4
  22.1 0.0 copy-start
  22.1 0.0 copy-start.3
  22.1 0.0 copy-start.5
  22.1 0.0 copy-start.1
  22.2 0.0 copy-start.2
  22.2 0.0 copy-start.6
  22.2 0.9 %collective-permute-done.5.rest_5_ = bf16[512,128]{1,0:T(8,128)(2,1)S(1)} collective-permute-done((bf16[512,128]{1,0:T(8,128)(2,1)S(1)}, bf16[512,128]{1,0:T(8,128)(2,1)S(1)}, u32[]{:S(2)}, u32[]{:S(2)}) %collective-permute-start.5) | collective-permute-done | bytes 131104 | tf_op jit(solution)/shard_map/ppermute | solution.py:323
  23.1 0.4 collective-permute-done.7.rest_7_
  23.5 0.0 collective-permute-done.1.rest_1_
  23.5 0.0 collective-permute-done.3.rest_3_
  23.5 0.0 copy-done.4
  23.5 0.0 copy-done
  23.5 0.0 copy-done.3
  23.5 0.0 copy-done.5
  23.5 0.0 copy-done.1
  23.5 0.0 copy-done.2
  23.5 2.9 %shard_map.73 = (bf16[256,128]{1,0:T(8,128)(2,1)S(1)}, bf16[256,128]{1,0:T(8,128)(2,1)S(1)}, bf16[16,128,128]{2,1,0:T(8,128)(2,1)S(1)}, bf16[32,80,128]{2,1,0:T(8,128)(2,1)S(1)}) custom-call(s32[216]{0:T(256)S(1)} %copy-done.1, s32[216]{0:T(256)S(1)} %copy-done.2, s32[576]{0:T(1024)S(1)} %copy-done, s32[216]{0:T(256)S(1)} %copy-done.3, s32[216]{0:T(256)S(1)} %copy-done.4, ...), custom_call_target="tpu_custom_call" | custom-call | tf_op jit(solution)/shard_map/pallas_call | solution.py:388
  26.4 0.0 copy-done.6
  26.4 0.0 copy-start.8
  26.4 0.0 copy-start.7
  26.5 1.6 %collective-permute-start.18 = (bf16[256,512]{1,0:T(8,128)(2,1)S(1)}, bf16[256,512]{1,0:T(8,128)(2,1)S(1)}, u32[]{:S(2)}, u32[]{:S(2)}) collective-permute-start(bf16[256,512]{1,0:T(8,128)(2,1)S(1)} %get-tuple-element.61), channel_id=1, source_target_pairs={{0,2},{1,3},{2,0},{3,1},{4,6},{5,7},{6,4},{7,5},{8,10},{9,11},{10,... | collective-permute-start | bytes 786440 | tf_op jit(solution)/shard_map/ppermute | solution.py:326
  28.1 0.0 copy-done.8
  28.1 3.5 %collective-permute-start.10 = (bf16[256,128]{1,0:T(8,128)(2,1)S(1)}, bf16[256,128]{1,0:T(8,128)(2,1)S(1)}, u32[]{:S(2)}, u32[]{:S(2)}) collective-permute-start(bf16[256,128]{1,0:T(8,128)(2,1)S(1)} %copy-done.8), channel_id=1, source_target_pairs={{0,16},{1,20},{2,18},{3,22},{4,17},{5,21},{6,19},{7,23},{8,24},{9,... | collective-permute-start | bytes 196616 | tf_op jit(solution)/shard_map/ppermute | solution.py:317
  31.6 0.0 copy-done.7
  31.6 0.5 collective-permute-start.11
  32.1 2.5 %collective-permute-done.10.rest_2_ = bf16[256,128]{1,0:T(8,128)(2,1)S(1)} collective-permute-done((bf16[256,128]{1,0:T(8,128)(2,1)S(1)}, bf16[256,128]{1,0:T(8,128)(2,1)S(1)}, u32[]{:S(2)}, u32[]{:S(2)}) %collective-permute-start.10) | collective-permute-done | bytes 65568 | tf_op jit(solution)/shard_map/ppermute | solution.py:317
  34.6 3.0 %collective-permute-done.11.rest_3_ = bf16[256,128]{1,0:T(8,128)(2,1)S(1)} collective-permute-done((bf16[256,128]{1,0:T(8,128)(2,1)S(1)}, bf16[256,128]{1,0:T(8,128)(2,1)S(1)}, u32[]{:S(2)}, u32[]{:S(2)}) %collective-permute-start.11) | collective-permute-done | bytes 65568 | tf_op jit(solution)/shard_map/ppermute | solution.py:317
  37.6 3.7 %shard_map.74 = (bf16[256,128]{1,0:T(8,128)(2,1)S(1)}, bf16[256,128]{1,0:T(8,128)(2,1)S(1)}) custom-call(s32[216]{0:T(256)S(1)} %copy-done.1, s32[216]{0:T(256)S(1)} %copy-done.2, s32[576]{0:T(1024)S(1)} %copy-done, s32[216]{0:T(256)S(1)} %copy-done.3, s32[216]{0:T(256)S(1)} %copy-done.4, s32[2]{0:T(128)S(1)} %copy-done.5, ...), custom_call_target="tpu_custom_call" | custom-call | tf_op jit(solution)/shard_map/pallas_call | solution.py:388
  41.3 1.1 %collective-permute-start.12 = (bf16[256,128]{1,0:T(8,128)(2,1)S(1)}, bf16[256,128]{1,0:T(8,128)(2,1)S(1)}, u32[]{:S(2)}, u32[]{:S(2)}) collective-permute-start(bf16[256,128]{1,0:T(8,128)(2,1)S(1)} %get-tuple-element.58), channel_id=1, source_target_pairs={{0,16},{1,20},{2,18},{3,22},{4,17},{5,21},{6,19},{7,23},{8,24},{9,... | collective-permute-start | bytes 196616 | tf_op jit(solution)/shard_map/ppermute | solution.py:317
  42.4 2.8 %collective-permute-start.13 = (bf16[256,128]{1,0:T(8,128)(2,1)S(1)}, bf16[256,128]{1,0:T(8,128)(2,1)S(1)}, u32[]{:S(2)}, u32[]{:S(2)}) collective-permute-start(bf16[256,128]{1,0:T(8,128)(2,1)S(1)} %get-tuple-element.59), channel_id=1, source_target_pairs={{0,24},{1,28},{2,26},{3,30},{4,25},{5,29},{6,27},{7,31},{8,16},{9,... | collective-permute-start | bytes 196616 | tf_op jit(solution)/shard_map/ppermute | solution.py:317
  45.2 0.7 %collective-permute-start.8 = (bf16[256,128]{1,0:T(8,128)(2,1)S(1)}, bf16[256,128]{1,0:T(8,128)(2,1)S(1)}, u32[]{:S(2)}, u32[]{:S(2)}) collective-permute-start(bf16[256,128]{1,0:T(8,128)(2,1)S(1)} %get-tuple-element.50), channel_id=1, source_target_pairs={{0,0},{1,4},{2,2},{3,6},{4,1},{5,5},{6,3},{7,7},{8,8},{9,12},{10,1... | collective-permute-start | bytes 196616 | tf_op jit(solution)/shard_map/ppermute | solution.py:317
  45.8 0.1 collective-permute-start.9
  45.9 0.9 %collective-permute-done.12.refs_2_ = bf16[256,128]{1,0:T(8,128)(2,1)S(1)} collective-permute-done((bf16[256,128]{1,0:T(8,128)(2,1)S(1)}, bf16[256,128]{1,0:T(8,128)(2,1)S(1)}, u32[]{:S(2)}, u32[]{:S(2)}) %collective-permute-start.12) | collective-permute-done | bytes 65568 | tf_op jit(solution)/shard_map/ppermute | solution.py:317
  46.8 4.3 %collective-permute-start.16 = (bf16[256,128]{1,0:T(8,128)(2,1)S(1)}, bf16[256,128]{1,0:T(8,128)(2,1)S(1)}, u32[]{:S(2)}, u32[]{:S(2)}) collective-permute-start(bf16[256,128]{1,0:T(8,128)(2,1)S(1)} %collective-permute-done.12.refs_2_), channel_id=1, source_target_pairs={{0,2},{1,3},{2,0},{3,1},{4,6},{5,7},{6,4},{7,5},{8,10},{9,11},{10,... | collective-permute-start | bytes 196616 | tf_op jit(solution)/shard_map/ppermute | solution.py:326
  51.0 0.0 collective-permute-done.13.refs_3_
  51.0 0.0 collective-permute-start.17
  51.1 0.0 collective-permute-done.8.refs_0_
  51.1 2.0 %collective-permute-start.14 = (bf16[256,128]{1,0:T(8,128)(2,1)S(1)}, bf16[256,128]{1,0:T(8,128)(2,1)S(1)}, u32[]{:S(2)}, u32[]{:S(2)}) collective-permute-start(bf16[256,128]{1,0:T(8,128)(2,1)S(1)} %collective-permute-done.8.refs_0_), channel_id=1, source_target_pairs={{0,2},{1,3},{2,0},{3,1},{4,6},{5,7},{6,4},{7,5},{8,10},{9,11},{10,... | collective-permute-start | bytes 196616 | tf_op jit(solution)/shard_map/ppermute | solution.py:326
  53.1 0.0 collective-permute-done.9.refs_1_
  53.1 0.1 collective-permute-start.15
  53.1 0.7 %collective-permute-done.16.refs_6_ = bf16[256,128]{1,0:T(8,128)(2,1)S(1)} collective-permute-done((bf16[256,128]{1,0:T(8,128)(2,1)S(1)}, bf16[256,128]{1,0:T(8,128)(2,1)S(1)}, u32[]{:S(2)}, u32[]{:S(2)}) %collective-permute-start.16) | collective-permute-done | bytes 65568 | tf_op jit(solution)/shard_map/ppermute | solution.py:326
  53.8 2.2 %collective-permute-done.17.refs_7_ = bf16[256,128]{1,0:T(8,128)(2,1)S(1)} collective-permute-done((bf16[256,128]{1,0:T(8,128)(2,1)S(1)}, bf16[256,128]{1,0:T(8,128)(2,1)S(1)}, u32[]{:S(2)}, u32[]{:S(2)}) %collective-permute-start.17) | collective-permute-done | bytes 65568 | tf_op jit(solution)/shard_map/ppermute | solution.py:326
  56.0 0.8 %collective-permute-done.14.refs_4_ = bf16[256,128]{1,0:T(8,128)(2,1)S(1)} collective-permute-done((bf16[256,128]{1,0:T(8,128)(2,1)S(1)}, bf16[256,128]{1,0:T(8,128)(2,1)S(1)}, u32[]{:S(2)}, u32[]{:S(2)}) %collective-permute-start.14) | collective-permute-done | bytes 65568 | tf_op jit(solution)/shard_map/ppermute | solution.py:326
  56.8 1.3 %collective-permute-done.15.refs_5_ = bf16[256,128]{1,0:T(8,128)(2,1)S(1)} collective-permute-done((bf16[256,128]{1,0:T(8,128)(2,1)S(1)}, bf16[256,128]{1,0:T(8,128)(2,1)S(1)}, u32[]{:S(2)}, u32[]{:S(2)}) %collective-permute-start.15) | collective-permute-done | bytes 65568 | tf_op jit(solution)/shard_map/ppermute | solution.py:326
  58.2 0.0 collective-permute-done.18.refs_9_
  58.2 0.4 shard_map.75
  58.6 0.1 collective-permute-start.19
  58.7 1.5 %collective-permute-done.19.refs_10_ = bf16[512,256]{1,0:T(8,128)(2,1)S(1)} collective-permute-done((bf16[512,256]{1,0:T(8,128)(2,1)S(1)}, bf16[512,256]{1,0:T(8,128)(2,1)S(1)}, u32[]{:S(2)}, u32[]{:S(2)}) %collective-permute-start.19) | collective-permute-done | bytes 262176 | tf_op jit(solution)/shard_map/ppermute | solution.py:326
  60.2 1.1 %shard_map.76 = bf16[512,256]{1,0:T(8,128)(2,1)} custom-call(bf16[256,128]{1,0:T(8,128)(2,1)S(1)} %collective-permute-done.8.refs_0_, bf16[256,128]{1,0:T(8,128)(2,1)S(1)} %collective-permute-done.9.refs_1_, bf16[256,128]{1,0:T(8,128)(2,1)S(1)} %collective-permute-done.12.refs_2_, bf16[256,128]{1,0:T(8,128)(2,1)S(1)} %collective-permute-done.13.refs_3_, ...), custom_call_target="tpu_custom_call" | custom-call | tf_op jit(solution)/shard_map/pallas_call | solution.py:421
  (1 shorter events, 0.0 us)
Async XLA Ops:
  3.6 11.1 %collective-permute-start = (bf16[768,128]{1,0:T(8,128)(2,1)}, bf16[768,128]{1,0:T(8,128)(2,1)S(1)}, u32[]{:S(2)}, u32[]{:S(2)}) collective-permute-start(bf16[768,128]{1,0:T(8,128)(2,1)} %get-tuple-element.33), channel_id=1, source_target_pairs={{0,0},{1,4},{2,2},{3,6},{4,1},{5,5},{6,3},{7,7},{8,8},{9,12},{10,1... | collective-permute-start | bytes 589832 | tf_op jit(solution)/shard_map/ppermute | solution.py:317
  5.2 12.2 %collective-permute-start.2 = (bf16[768,128]{1,0:T(8,128)(2,1)}, bf16[768,128]{1,0:T(8,128)(2,1)S(1)}, u32[]{:S(2)}, u32[]{:S(2)}) collective-permute-start(bf16[768,128]{1,0:T(8,128)(2,1)} %get-tuple-element.47), channel_id=1, source_target_pairs={{0,8},{1,12},{2,10},{3,14},{4,9},{5,13},{6,11},{7,15},{8,0},{9,4},... | collective-permute-start | bytes 589832 | tf_op jit(solution)/shard_map/ppermute | solution.py:317
  8.2 9.2 %collective-permute-start.4 = (bf16[512,128]{1,0:T(8,128)(2,1)}, bf16[512,128]{1,0:T(8,128)(2,1)S(1)}, u32[]{:S(2)}, u32[]{:S(2)}) collective-permute-start(bf16[512,128]{1,0:T(8,128)(2,1)} %get-tuple-element.48), channel_id=1, source_target_pairs={{0,16},{1,20},{2,18},{3,22},{4,17},{5,21},{6,19},{7,23},{8,24},{9,... | collective-permute-start | bytes 393224 | tf_op jit(solution)/shard_map/ppermute | solution.py:317
  10.8 11.3 %collective-permute-start.6 = (bf16[512,128]{1,0:T(8,128)(2,1)}, bf16[512,128]{1,0:T(8,128)(2,1)S(1)}, u32[]{:S(2)}, u32[]{:S(2)}) collective-permute-start(bf16[512,128]{1,0:T(8,128)(2,1)} %get-tuple-element.49), channel_id=1, source_target_pairs={{0,24},{1,28},{2,26},{3,30},{4,25},{5,29},{6,27},{7,31},{8,16},{9,... | collective-permute-start | bytes 393224 | tf_op jit(solution)/shard_map/ppermute | solution.py:317
  14.7 8.7 %collective-permute-start.1 = (bf16[768,128]{1,0:T(8,128)(2,1)S(1)}, bf16[768,128]{1,0:T(8,128)(2,1)S(1)}, u32[]{:S(2)}, u32[]{:S(2)}) collective-permute-start(bf16[768,128]{1,0:T(8,128)(2,1)S(1)} %collective-permute-done.rest_0_.rest_8_), channel_id=1, source_target_pairs={{0,1},{1,0},{2,3},{3,2},{4,5},{5,4},{6,7},{7,6},{8,9},{9,8},{10,11... | collective-permute-start | bytes 589832 | tf_op jit(solution)/shard_map/ppermute | solution.py:323
  17.4 6.1 %collective-permute-start.3 = (bf16[768,128]{1,0:T(8,128)(2,1)S(1)}, bf16[768,128]{1,0:T(8,128)(2,1)S(1)}, u32[]{:S(2)}, u32[]{:S(2)}) collective-permute-start(bf16[768,128]{1,0:T(8,128)(2,1)S(1)} %collective-permute-done.2.rest_2_.rest_9_), channel_id=1, source_target_pairs={{0,1},{1,0},{2,3},{3,2},{4,5},{5,4},{6,7},{7,6},{8,9},{9,8},{10,11... | collective-permute-start | bytes 589832 | tf_op jit(solution)/shard_map/ppermute | solution.py:323
  17.4 5.6 %collective-permute-start.5 = (bf16[512,128]{1,0:T(8,128)(2,1)S(1)}, bf16[512,128]{1,0:T(8,128)(2,1)S(1)}, u32[]{:S(2)}, u32[]{:S(2)}) collective-permute-start(bf16[512,128]{1,0:T(8,128)(2,1)S(1)} %collective-permute-done.4.rest_4_), channel_id=1, source_target_pairs={{0,1},{1,0},{2,3},{3,2},{4,5},{5,4},{6,7},{7,6},{8,9},{9,8},{10,11... | collective-permute-start | bytes 393224 | tf_op jit(solution)/shard_map/ppermute | solution.py:323
  22.1 1.3 %collective-permute-start.7 = (bf16[512,128]{1,0:T(8,128)(2,1)S(1)}, bf16[512,128]{1,0:T(8,128)(2,1)S(1)}, u32[]{:S(2)}, u32[]{:S(2)}) collective-permute-start(bf16[512,128]{1,0:T(8,128)(2,1)S(1)} %collective-permute-done.6.rest_6_), channel_id=1, source_target_pairs={{0,1},{1,0},{2,3},{3,2},{4,5},{5,4},{6,7},{7,6},{8,9},{9,8},{10,11... | collective-permute-start | bytes 393224 | tf_op jit(solution)/shard_map/ppermute | solution.py:323
  22.1 1.4 %copy-start.4 = (s32[216]{0:T(256)S(1)}, s32[216]{0:T(256)}, u32[]{:S(2)}) copy-start(s32[216]{0:T(256)} %get-tuple-element.44.first) | copy-start | bytes 2596
  22.1 1.4 %copy-start = (s32[576]{0:T(1024)S(1)}, s32[576]{0:T(1024)}, u32[]{:S(2)}) copy-start(s32[576]{0:T(1024)} %get-tuple-element.42.which) | copy-start | bytes 6916
  22.1 1.4 %copy-start.3 = (s32[216]{0:T(256)S(1)}, s32[216]{0:T(256)}, u32[]{:S(2)}) copy-start(s32[216]{0:T(256)} %get-tuple-element.43.valid) | copy-start | bytes 2596
  22.1 1.4 %copy-start.5 = (s32[2]{0:T(128)S(1)}, s32[2]{0:T(128)}, u32[]{:S(2)}) copy-start(s32[2]{0:T(128)} %get-tuple-element.45.steps) | copy-start | bytes 28
  22.1 1.4 %copy-start.1 = (s32[216]{0:T(256)S(1)}, s32[216]{0:T(256)}, u32[]{:S(2)}) copy-start(s32[216]{0:T(256)} %get-tuple-element.40.who) | copy-start | bytes 2596
  22.2 1.4 %copy-start.2 = (s32[216]{0:T(256)S(1)}, s32[216]{0:T(256)}, u32[]{:S(2)}) copy-start(s32[216]{0:T(256)} %get-tuple-element.41.where) | copy-start | bytes 2596
  22.2 4.3 %copy-start.6 = (bf16[256,1024]{1,0:T(8,128)(2,1)S(1)}, bf16[256,1024]{1,0:T(8,128)(2,1)}, u32[]{:S(2)}) copy-start(bf16[256,1024]{1,0:T(8,128)(2,1)} %param.11) | copy-start | bytes 1572868
  26.4 1.6 %copy-start.8 = (bf16[256,128]{1,0:T(8,128)(2,1)S(1)}, bf16[256,128]{1,0:T(8,128)(2,1)}, u32[]{:S(2)}) copy-start(bf16[256,128]{1,0:T(8,128)(2,1)} %get-tuple-element.56) | copy-start | bytes 196612
  26.4 5.1 %copy-start.7 = (bf16[256,128]{1,0:T(8,128)(2,1)S(1)}, bf16[256,128]{1,0:T(8,128)(2,1)}, u32[]{:S(2)}) copy-start(bf16[256,128]{1,0:T(8,128)(2,1)} %get-tuple-element.57) | copy-start | bytes 196612
  26.5 31.7 %collective-permute-start.18 = (bf16[256,512]{1,0:T(8,128)(2,1)S(1)}, bf16[256,512]{1,0:T(8,128)(2,1)S(1)}, u32[]{:S(2)}, u32[]{:S(2)}) collective-permute-start(bf16[256,512]{1,0:T(8,128)(2,1)S(1)} %get-tuple-element.61), channel_id=1, source_target_pairs={{0,2},{1,3},{2,0},{3,1},{4,6},{5,7},{6,4},{7,5},{8,10},{9,11},{10,... | collective-permute-start | bytes 786440 | tf_op jit(solution)/shard_map/ppermute | solution.py:326
  28.1 6.5 %collective-permute-start.10 = (bf16[256,128]{1,0:T(8,128)(2,1)S(1)}, bf16[256,128]{1,0:T(8,128)(2,1)S(1)}, u32[]{:S(2)}, u32[]{:S(2)}) collective-permute-start(bf16[256,128]{1,0:T(8,128)(2,1)S(1)} %copy-done.8), channel_id=1, source_target_pairs={{0,16},{1,20},{2,18},{3,22},{4,17},{5,21},{6,19},{7,23},{8,24},{9,... | collective-permute-start | bytes 196616 | tf_op jit(solution)/shard_map/ppermute | solution.py:317
  31.6 6.1 %collective-permute-start.11 = (bf16[256,128]{1,0:T(8,128)(2,1)S(1)}, bf16[256,128]{1,0:T(8,128)(2,1)S(1)}, u32[]{:S(2)}, u32[]{:S(2)}) collective-permute-start(bf16[256,128]{1,0:T(8,128)(2,1)S(1)} %copy-done.7), channel_id=1, source_target_pairs={{0,24},{1,28},{2,26},{3,30},{4,25},{5,29},{6,27},{7,31},{8,16},{9,... | collective-permute-start | bytes 196616 | tf_op jit(solution)/shard_map/ppermute | solution.py:317
  41.3 5.5 %collective-permute-start.12 = (bf16[256,128]{1,0:T(8,128)(2,1)S(1)}, bf16[256,128]{1,0:T(8,128)(2,1)S(1)}, u32[]{:S(2)}, u32[]{:S(2)}) collective-permute-start(bf16[256,128]{1,0:T(8,128)(2,1)S(1)} %get-tuple-element.58), channel_id=1, source_target_pairs={{0,16},{1,20},{2,18},{3,22},{4,17},{5,21},{6,19},{7,23},{8,24},{9,... | collective-permute-start | bytes 196616 | tf_op jit(solution)/shard_map/ppermute | solution.py:317
  42.4 8.6 %collective-permute-start.13 = (bf16[256,128]{1,0:T(8,128)(2,1)S(1)}, bf16[256,128]{1,0:T(8,128)(2,1)S(1)}, u32[]{:S(2)}, u32[]{:S(2)}) collective-permute-start(bf16[256,128]{1,0:T(8,128)(2,1)S(1)} %get-tuple-element.59), channel_id=1, source_target_pairs={{0,24},{1,28},{2,26},{3,30},{4,25},{5,29},{6,27},{7,31},{8,16},{9,... | collective-permute-start | bytes 196616 | tf_op jit(solution)/shard_map/ppermute | solution.py:317
  45.2 5.9 %collective-permute-start.8 = (bf16[256,128]{1,0:T(8,128)(2,1)S(1)}, bf16[256,128]{1,0:T(8,128)(2,1)S(1)}, u32[]{:S(2)}, u32[]{:S(2)}) collective-permute-start(bf16[256,128]{1,0:T(8,128)(2,1)S(1)} %get-tuple-element.50), channel_id=1, source_target_pairs={{0,0},{1,4},{2,2},{3,6},{4,1},{5,5},{6,3},{7,7},{8,8},{9,12},{10,1... | collective-permute-start | bytes 196616 | tf_op jit(solution)/shard_map/ppermute | solution.py:317
  45.8 7.2 %collective-permute-start.9 = (bf16[256,128]{1,0:T(8,128)(2,1)S(1)}, bf16[256,128]{1,0:T(8,128)(2,1)S(1)}, u32[]{:S(2)}, u32[]{:S(2)}) collective-permute-start(bf16[256,128]{1,0:T(8,128)(2,1)S(1)} %get-tuple-element.51), channel_id=1, source_target_pairs={{0,8},{1,12},{2,10},{3,14},{4,9},{5,13},{6,11},{7,15},{8,0},{9,4},... | collective-permute-start | bytes 196616 | tf_op jit(solution)/shard_map/ppermute | solution.py:317
  46.8 7.0 %collective-permute-start.16 = (bf16[256,128]{1,0:T(8,128)(2,1)S(1)}, bf16[256,128]{1,0:T(8,128)(2,1)S(1)}, u32[]{:S(2)}, u32[]{:S(2)}) collective-permute-start(bf16[256,128]{1,0:T(8,128)(2,1)S(1)} %collective-permute-done.12.refs_2_), channel_id=1, source_target_pairs={{0,2},{1,3},{2,0},{3,1},{4,6},{5,7},{6,4},{7,5},{8,10},{9,11},{10,... | collective-permute-start | bytes 196616 | tf_op jit(solution)/shard_map/ppermute | solution.py:326
  51.0 5.0 %collective-permute-start.17 = (bf16[256,128]{1,0:T(8,128)(2,1)S(1)}, bf16[256,128]{1,0:T(8,128)(2,1)S(1)}, u32[]{:S(2)}, u32[]{:S(2)}) collective-permute-start(bf16[256,128]{1,0:T(8,128)(2,1)S(1)} %collective-permute-done.13.refs_3_), channel_id=1, source_target_pairs={{0,2},{1,3},{2,0},{3,1},{4,6},{5,7},{6,4},{7,5},{8,10},{9,11},{10,... | collective-permute-start | bytes 196616 | tf_op jit(solution)/shard_map/ppermute | solution.py:326
  51.1 5.8 %collective-permute-start.14 = (bf16[256,128]{1,0:T(8,128)(2,1)S(1)}, bf16[256,128]{1,0:T(8,128)(2,1)S(1)}, u32[]{:S(2)}, u32[]{:S(2)}) collective-permute-start(bf16[256,128]{1,0:T(8,128)(2,1)S(1)} %collective-permute-done.8.refs_0_), channel_id=1, source_target_pairs={{0,2},{1,3},{2,0},{3,1},{4,6},{5,7},{6,4},{7,5},{8,10},{9,11},{10,... | collective-permute-start | bytes 196616 | tf_op jit(solution)/shard_map/ppermute | solution.py:326
  53.1 5.1 %collective-permute-start.15 = (bf16[256,128]{1,0:T(8,128)(2,1)S(1)}, bf16[256,128]{1,0:T(8,128)(2,1)S(1)}, u32[]{:S(2)}, u32[]{:S(2)}) collective-permute-start(bf16[256,128]{1,0:T(8,128)(2,1)S(1)} %collective-permute-done.9.refs_1_), channel_id=1, source_target_pairs={{0,2},{1,3},{2,0},{3,1},{4,6},{5,7},{6,4},{7,5},{8,10},{9,11},{10,... | collective-permute-start | bytes 196616 | tf_op jit(solution)/shard_map/ppermute | solution.py:326
  58.6 1.6 %collective-permute-start.19 = (bf16[512,256]{1,0:T(8,128)(2,1)S(1)}, bf16[512,256]{1,0:T(8,128)(2,1)S(1)}, u32[]{:S(2)}, u32[]{:S(2)}) collective-permute-start(bf16[512,256]{1,0:T(8,128)(2,1)S(1)} %shard_map.75), channel_id=1, source_target_pairs={{0,1},{1,0},{2,3},{3,2},{4,5},{5,4},{6,7},{7,6},{8,9},{9,8},{10,11... | collective-permute-start | bytes 786440 | tf_op jit(solution)/shard_map/ppermute | solution.py:326
where the time goes:
time: 61.5 us; the launch traced here: 61.2 us
  starting transfers between devices  31.2 us (51%)
  Pallas kernels  15.5 us (25%)
  waiting for transfers between devices  14.3 us (23%)
    ppermute x10, starting transfers between devices, turn(): return lax.ppermute(x, both, pairs)  15.8 us
    ppermute x6, starting transfers between devices, head_swap(): lax.ppermute(x, 'head', [(h, h ^ j) for h in range(groups)])  8.03 us
    ppermute x4, starting transfers between devices, spread(): return lax.ppermute(x, both, pairs) if e else x  7.38 us
    pallas_call x2, Pallas kernels, body(): pl.pallas_call(functools.partial(attend_kernel, part, per, cap, len(kv),...  6.57 us
    ppermute x6, waiting for transfers between devices, head_swap(): lax.ppermute(x, 'head', [(h, h ^ j) for h in range(groups)])  6.53 us
    ppermute x10, waiting for transfers between devices, turn(): return lax.ppermute(x, both, pairs)  6.44 us
    pallas_call x1, Pallas kernels, body(): pl.pallas_call(functools.partial(list_kernel, inner, heads, per, cap, par...  3.87 us
    pallas_call x1, Pallas kernels, body(): pl.pallas_call(functools.partial(proj_kernel, inner, heads, near), out_sh...  3.59 us
  transfers between devices with their start and end apart: 20, of which 10 were waited for; matrix products, arithmetic and copies ran while one was open for 0% of the time, Pallas kernels for 12%

commit v1 on v0

--- a/solution.py
+++ b/solution.py
@@ -309,9 +309,9 @@
         def index(a, b, h):
             return (a * inner + b) * groups + h
 
-        def turn(x, j):
+        def turn(x, j, g=0):
             pairs = [
-                (index(a, b, h), index(a ^ j, (b & ~1) | (h & 1), (h & ~1) | (b & 1)))
+                (index(a, b, h), index(a ^ j, (b & ~1) | (h & 1), ((h & ~1) | (b & 1)) ^ g))
                 for a, b, h in places
             ]
             return lax.ppermute(x, both, pairs)
@@ -367,6 +367,12 @@
             name="block_lists",
         )(block_mask, block_order)
         queries = msgs[heads:]
+        h = lax.axis_index("head")
+        w_out, msgs = lax.optimization_barrier((w_out, msgs))
+        w_cols = []
+        for g in range(0, groups, 2):
+            share = lax.dynamic_slice_in_dim(w_out, (h // 2 ^ g // 2) * 2 * cols, 2 * cols, axis=1)
+            w_cols.append(head_swap(share, g))
         got[0], tables = lax.optimization_barrier((got[0], tables))
         for j in range(near, heads):
             late[j] = turn(queries[j - near], j)
@@ -402,20 +408,14 @@
             )(*tables, *kv, *queries)
             o += made[:near]
             if part == 0:
-                h = lax.axis_index("head")
-                w_out, kv = lax.optimization_barrier((w_out, made[near:]))
-                w_cols = []
-                for g in range(0, groups, 2):
-                    start = (h // 2 ^ g // 2) * 2 * cols
-                    share = lax.dynamic_slice_in_dim(w_out, start, 2 * cols, axis=1)
-                    w_cols.append(head_swap(share, g))
+                kv = made[near:]
         mine = [None] * heads
         for j in reversed(range(heads)):
             mine[j] = turn(o[j], j)
         pieces = []
         for g in range(0, groups, 2):
             for j in range(heads):
-                pieces.append(head_swap(mine[j], g))
+                pieces.append(head_swap(mine[j], g) if j >= near or not g else turn(o[j], j, g))
 
         def out(other, *more):
             return pl.pallas_call(

time: 61.5 us -> 56.8 us (0.924)
  waiting for transfers between devices: 14.3 us -> 9.89 us
  starting transfers between devices: 31.2 us -> 30.4 us
    ppermute x6 -> x4, waiting for transfers between devices: 6.53 us -> 1.87 us  [head_swap(): lax.ppermute(x, 'head', [(h, h ^ j) for h in range(groups)])]
    ppermute x6 -> x4, starting transfers between devices: 8.03 us -> 6.39 us  [head_swap(): lax.ppermute(x, 'head', [(h, h ^ j) for h in range(groups)])]
    ppermute x10 -> x12, waiting for transfers between devices: 6.44 us -> 8 us  [turn(): return lax.ppermute(x, both, pairs)]
    ppermute x10 -> x12, starting transfers between devices: 15.8 us -> 17.2 us  [turn(): return lax.ppermute(x, both, pairs)]
    ppermute x4, waiting for transfers between devices: 1.28 us -> 0.01 us  [spread(): return lax.ppermute(x, both, pairs) if e else x]
  transfers between devices with their start and end apart: 20 -> 20, of which waited for: 10 -> 6; matrix products, arithmetic and copies ran while one was open for 0% -> 0% of each run, Pallas kernels for 12% -> 19%
where the time goes in v1:
time: 56.8 us; the launch traced here: 56 us
  starting transfers between devices  30.4 us (54%)
  Pallas kernels  15.5 us (27%)
  waiting for transfers between devices  9.89 us (17%)
    ppermute x12, starting transfers between devices, turn(): return lax.ppermute(x, both, pairs)  17.2 us
    ppermute x12, waiting for transfers between devices, turn(): return lax.ppermute(x, both, pairs)  8 us
    ppermute x4, starting transfers between devices, spread(): return lax.ppermute(x, both, pairs) if e else x  6.77 us
    pallas_call x2, Pallas kernels, body(): pl.pallas_call(functools.partial(attend_kernel, part, per, cap, len(kv),...  6.57 us
    ppermute x4, starting transfers between devices, head_swap(): lax.ppermute(x, 'head', [(h, h ^ j) for h in range(groups)])  6.39 us
    pallas_call x1, Pallas kernels, body(): pl.pallas_call(functools.partial(list_kernel, inner, heads, per, cap, par...  3.87 us
    pallas_call x1, Pallas kernels, body(): pl.pallas_call(functools.partial(proj_kernel, inner, heads, near), out_sh...  3.65 us
    ppermute x4, waiting for transfers between devices, head_swap(): lax.ppermute(x, 'head', [(h, h ^ j) for h in range(groups)])  1.87 us
  transfers between devices with their start and end apart: 20, of which 6 were waited for; matrix products, arithmetic and copies ran while one was open for 0% of the time, Pallas kernels for 19%

profile of v1, /device:TPU:0, one launch (start us, length us, event | category | flops | bytes accessed | tf_op | source)
XLA Modules:
  0.0 56.0 jit_solution(12808482239453227077)
XLA Ops:
  0.0 0.0 copy-start.6
  0.0 3.6 %proj.1 = (bf16[768,128]{1,0:T(8,128)(2,1)}, bf16[768,128]{1,0:T(8,128)(2,1)}, bf16[512,128]{1,0:T(8,128)(2,1)}, bf16[512,128]{1,0:T(8,128)(2,1)}, bf16[256,128]{1,0:T(8,128)(2,1)}, /*index=5*/bf16[256,128]{1,0:T(8,128)(2,1)}) custom-call(bf16[512,1024]{1,0:T(8,128)(2,1)} %tok_in.1, bf16[1024,256]{1,0:T(8,128)(2,1)} %wk_in.1, bf16[1024,256]{1,0:T(8,128)(2,1)} %wv_in.1, ...), custom_call_target="tpu_custom_call" | custom-call | tf_op jit(solution)/shard_map/proj/pallas_call | solution.py:331
  3.7 1.6 %collective-permute-start = (bf16[768,128]{1,0:T(8,128)(2,1)}, bf16[768,128]{1,0:T(8,128)(2,1)S(1)}, u32[]{:S(2)}, u32[]{:S(2)}) collective-permute-start(bf16[768,128]{1,0:T(8,128)(2,1)} %get-tuple-element.31), channel_id=1, source_target_pairs={{0,0},{1,4},{2,2},{3,6},{4,1},{5,5},{6,3},{7,7},{8,8},{9,12},{10,1... | collective-permute-start | bytes 589832 | tf_op jit(solution)/shard_map/ppermute | solution.py:317
  5.2 3.1 %collective-permute-start.2 = (bf16[768,128]{1,0:T(8,128)(2,1)}, bf16[768,128]{1,0:T(8,128)(2,1)S(1)}, u32[]{:S(2)}, u32[]{:S(2)}) collective-permute-start(bf16[768,128]{1,0:T(8,128)(2,1)} %get-tuple-element.45), channel_id=1, source_target_pairs={{0,8},{1,12},{2,10},{3,14},{4,9},{5,13},{6,11},{7,15},{8,0},{9,4},... | collective-permute-start | bytes 589832 | tf_op jit(solution)/shard_map/ppermute | solution.py:317
  8.3 2.6 %collective-permute-start.4 = (bf16[512,128]{1,0:T(8,128)(2,1)}, bf16[512,128]{1,0:T(8,128)(2,1)S(1)}, u32[]{:S(2)}, u32[]{:S(2)}) collective-permute-start(bf16[512,128]{1,0:T(8,128)(2,1)} %get-tuple-element.46), channel_id=1, source_target_pairs={{0,16},{1,20},{2,18},{3,22},{4,17},{5,21},{6,19},{7,23},{8,24},{9,... | collective-permute-start | bytes 393224 | tf_op jit(solution)/shard_map/ppermute | solution.py:317
  10.9 0.0 collective-permute-start.6
  10.9 3.9 %block_lists.1 = (s32[216]{0:T(256)}, s32[216]{0:T(256)}, s32[576]{0:T(1024)}, s32[216]{0:T(256)}, s32[216]{0:T(256)}, /*index=5*/s32[2]{0:T(128)}) custom-call(s32[32,32]{1,0:T(8,128)} %mask.1, s32[32]{0:T(128)} %order.1), custom_call_target="tpu_custom_call" | custom-call | tf_op jit(solution)/shard_map/block_lists/pallas_call | solution.py:350
  14.8 1.2 %collective-permute-done.4.rest_4_ = bf16[512,128]{1,0:T(8,128)(2,1)S(1)} collective-permute-done((bf16[512,128]{1,0:T(8,128)(2,1)}, bf16[512,128]{1,0:T(8,128)(2,1)S(1)}, u32[]{:S(2)}, u32[]{:S(2)}) %collective-permute-start.4) | collective-permute-done | bytes 131104 | tf_op jit(solution)/shard_map/ppermute | solution.py:317
  16.0 6.2 %collective-permute-start.5 = (bf16[512,128]{1,0:T(8,128)(2,1)S(1)}, bf16[512,128]{1,0:T(8,128)(2,1)S(1)}, u32[]{:S(2)}, u32[]{:S(2)}) collective-permute-start(bf16[512,128]{1,0:T(8,128)(2,1)S(1)} %collective-permute-done.4.rest_4_), channel_id=1, source_target_pairs={{0,1},{1,0},{2,3},{3,2},{4,5},{5,4},{6,7},{7,6},{8,9},{9,8},{10,11... | collective-permute-start | bytes 393224 | tf_op jit(solution)/shard_map/ppermute | solution.py:323
  22.2 0.0 collective-permute-done.6.rest_6_
  22.2 0.0 collective-permute-start.7
  22.2 0.0 collective-permute-done.rest_0_.rest_8_
  22.2 0.0 copy-start.8
  22.2 0.0 copy-start.7
  22.2 0.5 collective-permute-start.1
  22.7 0.0 collective-permute-done.2.rest_2_.rest_9_
  22.7 0.1 collective-permute-start.3
  22.8 0.0 copy-done.6
  22.8 0.0 copy-start
  22.8 0.0 copy-start.2
  22.8 0.0 copy-start.3
  22.8 0.0 copy-start.4
  22.9 0.0 copy-start.1
  22.9 0.0 copy-start.5
  22.9 1.6 %collective-permute-start.18 = (bf16[256,512]{1,0:T(8,128)(2,1)S(1)}, bf16[256,512]{1,0:T(8,128)(2,1)S(1)}, u32[]{:S(2)}, u32[]{:S(2)}) collective-permute-start(bf16[256,512]{1,0:T(8,128)(2,1)S(1)} %get-tuple-element.57), channel_id=1, source_target_pairs={{0,2},{1,3},{2,0},{3,1},{4,6},{5,7},{6,4},{7,5},{8,10},{9,11},{10,... | collective-permute-start | bytes 786440 | tf_op jit(solution)/shard_map/ppermute | solution.py:326
  24.4 0.0 collective-permute-done.5.rest_5_
  24.4 0.0 copy-done.8
  24.4 2.9 %collective-permute-start.10 = (bf16[256,128]{1,0:T(8,128)(2,1)S(1)}, bf16[256,128]{1,0:T(8,128)(2,1)S(1)}, u32[]{:S(2)}, u32[]{:S(2)}) collective-permute-start(bf16[256,128]{1,0:T(8,128)(2,1)S(1)} %copy-done.8), channel_id=1, source_target_pairs={{0,16},{1,20},{2,18},{3,22},{4,17},{5,21},{6,19},{7,23},{8,24},{9,... | collective-permute-start | bytes 196616 | tf_op jit(solution)/shard_map/ppermute | solution.py:317
  27.4 0.0 collective-permute-done.7.rest_7_
  27.4 0.0 copy-done.7
  27.4 1.3 %collective-permute-start.11 = (bf16[256,128]{1,0:T(8,128)(2,1)S(1)}, bf16[256,128]{1,0:T(8,128)(2,1)S(1)}, u32[]{:S(2)}, u32[]{:S(2)}) collective-permute-start(bf16[256,128]{1,0:T(8,128)(2,1)S(1)} %copy-done.7), channel_id=1, source_target_pairs={{0,24},{1,28},{2,26},{3,30},{4,25},{5,29},{6,27},{7,31},{8,16},{9,... | collective-permute-start | bytes 196616 | tf_op jit(solution)/shard_map/ppermute | solution.py:317
  28.7 0.0 collective-permute-done.1.rest_1_
  28.7 0.0 collective-permute-done.3.rest_3_
  28.7 0.0 copy-done
  28.7 0.0 copy-done.2
  28.7 0.0 copy-done.3
  28.7 0.0 copy-done.4
  28.7 0.0 copy-done.1
  28.7 0.0 copy-done.5
  28.7 2.9 %shard_map.73 = (bf16[256,128]{1,0:T(8,128)(2,1)S(1)}, bf16[256,128]{1,0:T(8,128)(2,1)S(1)}, bf16[16,128,128]{2,1,0:T(8,128)(2,1)S(1)}, bf16[32,80,128]{2,1,0:T(8,128)(2,1)S(1)}) custom-call(s32[216]{0:T(256)S(1)} %copy-done.1, s32[216]{0:T(256)S(1)} %copy-done.2, s32[576]{0:T(1024)S(1)} %copy-done, s32[216]{0:T(256)S(1)} %copy-done.3, s32[216]{0:T(256)S(1)} %copy-done.4, ...), custom_call_target="tpu_custom_call" | custom-call | tf_op jit(solution)/shard_map/pallas_call | solution.py:394
  31.6 0.0 collective-permute-done.10.rest_2_
  31.7 2.2 %collective-permute-done.11.rest_3_ = bf16[256,128]{1,0:T(8,128)(2,1)S(1)} collective-permute-done((bf16[256,128]{1,0:T(8,128)(2,1)S(1)}, bf16[256,128]{1,0:T(8,128)(2,1)S(1)}, u32[]{:S(2)}, u32[]{:S(2)}) %collective-permute-start.11) | collective-permute-done | bytes 65568 | tf_op jit(solution)/shard_map/ppermute | solution.py:317
  33.9 3.7 %shard_map.74 = (bf16[256,128]{1,0:T(8,128)(2,1)S(1)}, bf16[256,128]{1,0:T(8,128)(2,1)S(1)}) custom-call(s32[216]{0:T(256)S(1)} %copy-done.1, s32[216]{0:T(256)S(1)} %copy-done.2, s32[576]{0:T(1024)S(1)} %copy-done, s32[216]{0:T(256)S(1)} %copy-done.3, s32[216]{0:T(256)S(1)} %copy-done.4, s32[2]{0:T(128)S(1)} %copy-done.5, ...), custom_call_target="tpu_custom_call" | custom-call | tf_op jit(solution)/shard_map/pallas_call | solution.py:394
  37.6 0.1 collective-permute-start.12
  37.6 3.5 %collective-permute-start.13 = (bf16[256,128]{1,0:T(8,128)(2,1)S(1)}, bf16[256,128]{1,0:T(8,128)(2,1)S(1)}, u32[]{:S(2)}, u32[]{:S(2)}) collective-permute-start(bf16[256,128]{1,0:T(8,128)(2,1)S(1)} %get-tuple-element.55), channel_id=1, source_target_pairs={{0,24},{1,28},{2,26},{3,30},{4,25},{5,29},{6,27},{7,31},{8,16},{9,... | collective-permute-start | bytes 196616 | tf_op jit(solution)/shard_map/ppermute | solution.py:317
  41.1 0.5 collective-permute-start.14
  41.6 0.7 %collective-permute-start.8 = (bf16[256,128]{1,0:T(8,128)(2,1)S(1)}, bf16[256,128]{1,0:T(8,128)(2,1)S(1)}, u32[]{:S(2)}, u32[]{:S(2)}) collective-permute-start(bf16[256,128]{1,0:T(8,128)(2,1)S(1)} %get-tuple-element.48), channel_id=1, source_target_pairs={{0,0},{1,4},{2,2},{3,6},{4,1},{5,5},{6,3},{7,7},{8,8},{9,12},{10,1... | collective-permute-start | bytes 196616 | tf_op jit(solution)/shard_map/ppermute | solution.py:317
  42.3 0.0 collective-permute-done.18.refs_9_
  42.3 1.0 %collective-permute-start.15 = (bf16[256,128]{1,0:T(8,128)(2,1)S(1)}, bf16[256,128]{1,0:T(8,128)(2,1)S(1)}, u32[]{:S(2)}, u32[]{:S(2)}) collective-permute-start(bf16[256,128]{1,0:T(8,128)(2,1)S(1)} %get-tuple-element.49), channel_id=1, source_target_pairs={{0,10},{1,14},{2,8},{3,12},{4,11},{5,15},{6,9},{7,13},{8,2},{9,6},... | collective-permute-start | bytes 196616 | tf_op jit(solution)/shard_map/ppermute | solution.py:317
  43.3 2.3 %collective-permute-done.12.refs_2_ = bf16[256,128]{1,0:T(8,128)(2,1)S(1)} collective-permute-done((bf16[256,128]{1,0:T(8,128)(2,1)S(1)}, bf16[256,128]{1,0:T(8,128)(2,1)S(1)}, u32[]{:S(2)}, u32[]{:S(2)}) %collective-permute-start.12) | collective-permute-done | bytes 65568 | tf_op jit(solution)/shard_map/ppermute | solution.py:317
  45.6 0.0 collective-permute-start.9
  45.6 0.0 collective-permute-done.13.refs_3_
  45.7 0.5 collective-permute-start.16
  46.2 0.0 collective-permute-done.14.refs_4_
  46.2 1.5 %collective-permute-start.17 = (bf16[256,128]{1,0:T(8,128)(2,1)S(1)}, bf16[256,128]{1,0:T(8,128)(2,1)S(1)}, u32[]{:S(2)}, u32[]{:S(2)}) collective-permute-start(bf16[256,128]{1,0:T(8,128)(2,1)S(1)} %collective-permute-done.13.refs_3_), channel_id=1, source_target_pairs={{0,2},{1,3},{2,0},{3,1},{4,6},{5,7},{6,4},{7,5},{8,10},{9,11},{10,... | collective-permute-start | bytes 196616 | tf_op jit(solution)/shard_map/ppermute | solution.py:326
  47.7 0.0 collective-permute-done.8.refs_0_
  47.7 0.0 collective-permute-done.15.refs_5_
  47.7 2.2 %collective-permute-done.9.refs_1_ = bf16[256,128]{1,0:T(8,128)(2,1)S(1)} collective-permute-done((bf16[256,128]{1,0:T(8,128)(2,1)S(1)}, bf16[256,128]{1,0:T(8,128)(2,1)S(1)}, u32[]{:S(2)}, u32[]{:S(2)}) %collective-permute-start.9) | collective-permute-done | bytes 65568 | tf_op jit(solution)/shard_map/ppermute | solution.py:317
  49.9 0.0 collective-permute-done.16.refs_6_
  49.9 0.7 %collective-permute-done.17.refs_7_ = bf16[256,128]{1,0:T(8,128)(2,1)S(1)} collective-permute-done((bf16[256,128]{1,0:T(8,128)(2,1)S(1)}, bf16[256,128]{1,0:T(8,128)(2,1)S(1)}, u32[]{:S(2)}, u32[]{:S(2)}) %collective-permute-start.17) | collective-permute-done | bytes 65568 | tf_op jit(solution)/shard_map/ppermute | solution.py:326
  50.6 0.4 shard_map.75
  51.0 2.8 %collective-permute-start.19 = (bf16[512,256]{1,0:T(8,128)(2,1)S(1)}, bf16[512,256]{1,0:T(8,128)(2,1)S(1)}, u32[]{:S(2)}, u32[]{:S(2)}) collective-permute-start(bf16[512,256]{1,0:T(8,128)(2,1)S(1)} %shard_map.75), channel_id=1, source_target_pairs={{0,1},{1,0},{2,3},{3,2},{4,5},{5,4},{6,7},{7,6},{8,9},{9,8},{10,11... | collective-permute-start | bytes 786440 | tf_op jit(solution)/shard_map/ppermute | solution.py:326
  53.8 1.2 %collective-permute-done.19.refs_10_ = bf16[512,256]{1,0:T(8,128)(2,1)S(1)} collective-permute-done((bf16[512,256]{1,0:T(8,128)(2,1)S(1)}, bf16[512,256]{1,0:T(8,128)(2,1)S(1)}, u32[]{:S(2)}, u32[]{:S(2)}) %collective-permute-start.19) | collective-permute-done | bytes 262176 | tf_op jit(solution)/shard_map/ppermute | solution.py:326
  55.0 1.1 %shard_map.76 = bf16[512,256]{1,0:T(8,128)(2,1)} custom-call(bf16[256,128]{1,0:T(8,128)(2,1)S(1)} %collective-permute-done.8.refs_0_, bf16[256,128]{1,0:T(8,128)(2,1)S(1)} %collective-permute-done.9.refs_1_, bf16[256,128]{1,0:T(8,128)(2,1)S(1)} %collective-permute-done.12.refs_2_, bf16[256,128]{1,0:T(8,128)(2,1)S(1)} %collective-permute-done.13.refs_3_, ...), custom_call_target="tpu_custom_call" | custom-call | tf_op jit(solution)/shard_map/pallas_call | solution.py:421
  (1 shorter events, 0.0 us)
Async XLA Ops:
  0.0 22.8 %copy-start.6 = (bf16[256,1024]{1,0:T(8,128)(2,1)S(1)}, bf16[256,1024]{1,0:T(8,128)(2,1)}, u32[]{:S(2)}) copy-start(bf16[256,1024]{1,0:T(8,128)(2,1)} %param.11) | copy-start | bytes 1572868
  3.7 18.5 %collective-permute-start = (bf16[768,128]{1,0:T(8,128)(2,1)}, bf16[768,128]{1,0:T(8,128)(2,1)S(1)}, u32[]{:S(2)}, u32[]{:S(2)}) collective-permute-start(bf16[768,128]{1,0:T(8,128)(2,1)} %get-tuple-element.31), channel_id=1, source_target_pairs={{0,0},{1,4},{2,2},{3,6},{4,1},{5,5},{6,3},{7,7},{8,8},{9,12},{10,1... | collective-permute-start | bytes 589832 | tf_op jit(solution)/shard_map/ppermute | solution.py:317
  5.2 17.4 %collective-permute-start.2 = (bf16[768,128]{1,0:T(8,128)(2,1)}, bf16[768,128]{1,0:T(8,128)(2,1)S(1)}, u32[]{:S(2)}, u32[]{:S(2)}) collective-permute-start(bf16[768,128]{1,0:T(8,128)(2,1)} %get-tuple-element.45), channel_id=1, source_target_pairs={{0,8},{1,12},{2,10},{3,14},{4,9},{5,13},{6,11},{7,15},{8,0},{9,4},... | collective-permute-start | bytes 589832 | tf_op jit(solution)/shard_map/ppermute | solution.py:317
  8.3 7.7 %collective-permute-start.4 = (bf16[512,128]{1,0:T(8,128)(2,1)}, bf16[512,128]{1,0:T(8,128)(2,1)S(1)}, u32[]{:S(2)}, u32[]{:S(2)}) collective-permute-start(bf16[512,128]{1,0:T(8,128)(2,1)} %get-tuple-element.46), channel_id=1, source_target_pairs={{0,16},{1,20},{2,18},{3,22},{4,17},{5,21},{6,19},{7,23},{8,24},{9,... | collective-permute-start | bytes 393224 | tf_op jit(solution)/shard_map/ppermute | solution.py:317
  10.9 11.3 %collective-permute-start.6 = (bf16[512,128]{1,0:T(8,128)(2,1)}, bf16[512,128]{1,0:T(8,128)(2,1)S(1)}, u32[]{:S(2)}, u32[]{:S(2)}) collective-permute-start(bf16[512,128]{1,0:T(8,128)(2,1)} %get-tuple-element.47), channel_id=1, source_target_pairs={{0,24},{1,28},{2,26},{3,30},{4,25},{5,29},{6,27},{7,31},{8,16},{9,... | collective-permute-start | bytes 393224 | tf_op jit(solution)/shard_map/ppermute | solution.py:317
  16.0 8.5 %collective-permute-start.5 = (bf16[512,128]{1,0:T(8,128)(2,1)S(1)}, bf16[512,128]{1,0:T(8,128)(2,1)S(1)}, u32[]{:S(2)}, u32[]{:S(2)}) collective-permute-start(bf16[512,128]{1,0:T(8,128)(2,1)S(1)} %collective-permute-done.4.rest_4_), channel_id=1, source_target_pairs={{0,1},{1,0},{2,3},{3,2},{4,5},{5,4},{6,7},{7,6},{8,9},{9,8},{10,11... | collective-permute-start | bytes 393224 | tf_op jit(solution)/shard_map/ppermute | solution.py:323
  22.2 5.2 %collective-permute-start.7 = (bf16[512,128]{1,0:T(8,128)(2,1)S(1)}, bf16[512,128]{1,0:T(8,128)(2,1)S(1)}, u32[]{:S(2)}, u32[]{:S(2)}) collective-permute-start(bf16[512,128]{1,0:T(8,128)(2,1)S(1)} %collective-permute-done.6.rest_6_), channel_id=1, source_target_pairs={{0,1},{1,0},{2,3},{3,2},{4,5},{5,4},{6,7},{7,6},{8,9},{9,8},{10,11... | collective-permute-start | bytes 393224 | tf_op jit(solution)/shard_map/ppermute | solution.py:323
  22.2 2.3 %copy-start.8 = (bf16[256,128]{1,0:T(8,128)(2,1)S(1)}, bf16[256,128]{1,0:T(8,128)(2,1)}, u32[]{:S(2)}) copy-start(bf16[256,128]{1,0:T(8,128)(2,1)} %get-tuple-element.52) | copy-start | bytes 196612
  22.2 5.2 %copy-start.7 = (bf16[256,128]{1,0:T(8,128)(2,1)S(1)}, bf16[256,128]{1,0:T(8,128)(2,1)}, u32[]{:S(2)}) copy-start(bf16[256,128]{1,0:T(8,128)(2,1)} %get-tuple-element.53) | copy-start | bytes 196612
  22.2 6.5 %collective-permute-start.1 = (bf16[768,128]{1,0:T(8,128)(2,1)S(1)}, bf16[768,128]{1,0:T(8,128)(2,1)S(1)}, u32[]{:S(2)}, u32[]{:S(2)}) collective-permute-start(bf16[768,128]{1,0:T(8,128)(2,1)S(1)} %collective-permute-done.rest_0_.rest_8_), channel_id=1, source_target_pairs={{0,1},{1,0},{2,3},{3,2},{4,5},{5,4},{6,7},{7,6},{8,9},{9,8},{10,11... | collective-permute-start | bytes 589832 | tf_op jit(solution)/shard_map/ppermute | solution.py:323
  22.7 6.0 %collective-permute-start.3 = (bf16[768,128]{1,0:T(8,128)(2,1)S(1)}, bf16[768,128]{1,0:T(8,128)(2,1)S(1)}, u32[]{:S(2)}, u32[]{:S(2)}) collective-permute-start(bf16[768,128]{1,0:T(8,128)(2,1)S(1)} %collective-permute-done.2.rest_2_.rest_9_), channel_id=1, source_target_pairs={{0,1},{1,0},{2,3},{3,2},{4,5},{5,4},{6,7},{7,6},{8,9},{9,8},{10,11... | collective-permute-start | bytes 589832 | tf_op jit(solution)/shard_map/ppermute | solution.py:323
  22.8 5.9 %copy-start = (s32[576]{0:T(1024)S(1)}, s32[576]{0:T(1024)}, u32[]{:S(2)}) copy-start(s32[576]{0:T(1024)} %get-tuple-element.40.which) | copy-start | bytes 6916
  22.8 5.9 %copy-start.2 = (s32[216]{0:T(256)S(1)}, s32[216]{0:T(256)}, u32[]{:S(2)}) copy-start(s32[216]{0:T(256)} %get-tuple-element.39.where) | copy-start | bytes 2596
  22.8 5.9 %copy-start.3 = (s32[216]{0:T(256)S(1)}, s32[216]{0:T(256)}, u32[]{:S(2)}) copy-start(s32[216]{0:T(256)} %get-tuple-element.41.valid) | copy-start | bytes 2596
  22.8 5.9 %copy-start.4 = (s32[216]{0:T(256)S(1)}, s32[216]{0:T(256)}, u32[]{:S(2)}) copy-start(s32[216]{0:T(256)} %get-tuple-element.42.first) | copy-start | bytes 2596
  22.9 5.9 %copy-start.1 = (s32[216]{0:T(256)S(1)}, s32[216]{0:T(256)}, u32[]{:S(2)}) copy-start(s32[216]{0:T(256)} %get-tuple-element.38.who) | copy-start | bytes 2596
  22.9 5.9 %copy-start.5 = (s32[2]{0:T(128)S(1)}, s32[2]{0:T(128)}, u32[]{:S(2)}) copy-start(s32[2]{0:T(128)} %get-tuple-element.43.steps) | copy-start | bytes 28
  22.9 19.4 %collective-permute-start.18 = (bf16[256,512]{1,0:T(8,128)(2,1)S(1)}, bf16[256,512]{1,0:T(8,128)(2,1)S(1)}, u32[]{:S(2)}, u32[]{:S(2)}) collective-permute-start(bf16[256,512]{1,0:T(8,128)(2,1)S(1)} %get-tuple-element.57), channel_id=1, source_target_pairs={{0,2},{1,3},{2,0},{3,1},{4,6},{5,7},{6,4},{7,5},{8,10},{9,11},{10,... | collective-permute-start | bytes 786440 | tf_op jit(solution)/shard_map/ppermute | solution.py:326
  24.4 7.2 %collective-permute-start.10 = (bf16[256,128]{1,0:T(8,128)(2,1)S(1)}, bf16[256,128]{1,0:T(8,128)(2,1)S(1)}, u32[]{:S(2)}, u32[]{:S(2)}) collective-permute-start(bf16[256,128]{1,0:T(8,128)(2,1)S(1)} %copy-done.8), channel_id=1, source_target_pairs={{0,16},{1,20},{2,18},{3,22},{4,17},{5,21},{6,19},{7,23},{8,24},{9,... | collective-permute-start | bytes 196616 | tf_op jit(solution)/shard_map/ppermute | solution.py:317
  27.4 6.5 %collective-permute-start.11 = (bf16[256,128]{1,0:T(8,128)(2,1)S(1)}, bf16[256,128]{1,0:T(8,128)(2,1)S(1)}, u32[]{:S(2)}, u32[]{:S(2)}) collective-permute-start(bf16[256,128]{1,0:T(8,128)(2,1)S(1)} %copy-done.7), channel_id=1, source_target_pairs={{0,24},{1,28},{2,26},{3,30},{4,25},{5,29},{6,27},{7,31},{8,16},{9,... | collective-permute-start | bytes 196616 | tf_op jit(solution)/shard_map/ppermute | solution.py:317
  37.6 8.1 %collective-permute-start.12 = (bf16[256,128]{1,0:T(8,128)(2,1)S(1)}, bf16[256,128]{1,0:T(8,128)(2,1)S(1)}, u32[]{:S(2)}, u32[]{:S(2)}) collective-permute-start(bf16[256,128]{1,0:T(8,128)(2,1)S(1)} %get-tuple-element.54), channel_id=1, source_target_pairs={{0,16},{1,20},{2,18},{3,22},{4,17},{5,21},{6,19},{7,23},{8,24},{9,... | collective-permute-start | bytes 196616 | tf_op jit(solution)/shard_map/ppermute | solution.py:317
  37.6 8.0 %collective-permute-start.13 = (bf16[256,128]{1,0:T(8,128)(2,1)S(1)}, bf16[256,128]{1,0:T(8,128)(2,1)S(1)}, u32[]{:S(2)}, u32[]{:S(2)}) collective-permute-start(bf16[256,128]{1,0:T(8,128)(2,1)S(1)} %get-tuple-element.55), channel_id=1, source_target_pairs={{0,24},{1,28},{2,26},{3,30},{4,25},{5,29},{6,27},{7,31},{8,16},{9,... | collective-permute-start | bytes 196616 | tf_op jit(solution)/shard_map/ppermute | solution.py:317
  41.1 5.1 %collective-permute-start.14 = (bf16[256,128]{1,0:T(8,128)(2,1)S(1)}, bf16[256,128]{1,0:T(8,128)(2,1)S(1)}, u32[]{:S(2)}, u32[]{:S(2)}) collective-permute-start(bf16[256,128]{1,0:T(8,128)(2,1)S(1)} %get-tuple-element.48), channel_id=1, source_target_pairs={{0,2},{1,6},{2,0},{3,4},{4,3},{5,7},{6,1},{7,5},{8,10},{9,14},{10,... | collective-permute-start | bytes 196616 | tf_op jit(solution)/shard_map/ppermute | solution.py:317
  41.6 6.0 %collective-permute-start.8 = (bf16[256,128]{1,0:T(8,128)(2,1)S(1)}, bf16[256,128]{1,0:T(8,128)(2,1)S(1)}, u32[]{:S(2)}, u32[]{:S(2)}) collective-permute-start(bf16[256,128]{1,0:T(8,128)(2,1)S(1)} %get-tuple-element.48), channel_id=1, source_target_pairs={{0,0},{1,4},{2,2},{3,6},{4,1},{5,5},{6,3},{7,7},{8,8},{9,12},{10,1... | collective-permute-start | bytes 196616 | tf_op jit(solution)/shard_map/ppermute | solution.py:317
  42.3 5.4 %collective-permute-start.15 = (bf16[256,128]{1,0:T(8,128)(2,1)S(1)}, bf16[256,128]{1,0:T(8,128)(2,1)S(1)}, u32[]{:S(2)}, u32[]{:S(2)}) collective-permute-start(bf16[256,128]{1,0:T(8,128)(2,1)S(1)} %get-tuple-element.49), channel_id=1, source_target_pairs={{0,10},{1,14},{2,8},{3,12},{4,11},{5,15},{6,9},{7,13},{8,2},{9,6},... | collective-permute-start | bytes 196616 | tf_op jit(solution)/shard_map/ppermute | solution.py:317
  45.6 4.3 %collective-permute-start.9 = (bf16[256,128]{1,0:T(8,128)(2,1)S(1)}, bf16[256,128]{1,0:T(8,128)(2,1)S(1)}, u32[]{:S(2)}, u32[]{:S(2)}) collective-permute-start(bf16[256,128]{1,0:T(8,128)(2,1)S(1)} %get-tuple-element.49), channel_id=1, source_target_pairs={{0,8},{1,12},{2,10},{3,14},{4,9},{5,13},{6,11},{7,15},{8,0},{9,4},... | collective-permute-start | bytes 196616 | tf_op jit(solution)/shard_map/ppermute | solution.py:317
  45.7 4.3 %collective-permute-start.16 = (bf16[256,128]{1,0:T(8,128)(2,1)S(1)}, bf16[256,128]{1,0:T(8,128)(2,1)S(1)}, u32[]{:S(2)}, u32[]{:S(2)}) collective-permute-start(bf16[256,128]{1,0:T(8,128)(2,1)S(1)} %collective-permute-done.12.refs_2_), channel_id=1, source_target_pairs={{0,2},{1,3},{2,0},{3,1},{4,6},{5,7},{6,4},{7,5},{8,10},{9,11},{10,... | collective-permute-start | bytes 196616 | tf_op jit(solution)/shard_map/ppermute | solution.py:326
  46.2 4.4 %collective-permute-start.17 = (bf16[256,128]{1,0:T(8,128)(2,1)S(1)}, bf16[256,128]{1,0:T(8,128)(2,1)S(1)}, u32[]{:S(2)}, u32[]{:S(2)}) collective-permute-start(bf16[256,128]{1,0:T(8,128)(2,1)S(1)} %collective-permute-done.13.refs_3_), channel_id=1, source_target_pairs={{0,2},{1,3},{2,0},{3,1},{4,6},{5,7},{6,4},{7,5},{8,10},{9,11},{10,... | collective-permute-start | bytes 196616 | tf_op jit(solution)/shard_map/ppermute | solution.py:326
  51.0 4.0 %collective-permute-start.19 = (bf16[512,256]{1,0:T(8,128)(2,1)S(1)}, bf16[512,256]{1,0:T(8,128)(2,1)S(1)}, u32[]{:S(2)}, u32[]{:S(2)}) collective-permute-start(bf16[512,256]{1,0:T(8,128)(2,1)S(1)} %shard_map.75), channel_id=1, source_target_pairs={{0,1},{1,0},{2,3},{3,2},{4,5},{5,4},{6,7},{7,6},{8,9},{9,8},{10,11... | collective-permute-start | bytes 786440 | tf_op jit(solution)/shard_map/ppermute | solution.py:326
